TPU v7x, 32 devices: a whole 2x2x4 slice. The times are simulated.
32 devices in a mesh: slab: 4 (over x, core), kt: 8 (over z, y).
Axes of the slice: x: 2, y: 2, z: 4, core: 2. Of those that a mesh axis runs over, the one named last changes fastest.
Arguments:
- energies: float32 [4], replicated, may hold values from -0.5 to 0.1
- onsite: float32 [8, 4, 384], P('kt', 'slab'), may hold values from -3.5 to -2.5
- hamiltonian: bfloat16 [8, 4, 2, 384, 384], P('kt', 'slab'), may hold values from -0.109375 to 0.109375
- hopping: bfloat16 [8, 4, 2, 384, 384], P('kt', 'slab'), may hold values from -0.15625 to 0.15625
- contact: bfloat16 [8, 2, 384, 384], P('kt'), may hold values from -2 to 2
- previous: bfloat16 [8, 4, 4, 2, 2, 384, 384], P('kt', None, 'slab'), may hold values from -4 to 4
- neighbours: int32 [8, 2], P('kt'), may hold values from 0 to 7, as said below
- mode_index: int32 [8, 2], P('kt'), may hold values from 0 to 3
- mode_strength: float32 [4], replicated, may hold values from 0.25 to 1
Outputs:
- retarded: bfloat16 [8, 4, 4, 2, 384, 384], P('kt', None, 'slab')
- lesser: bfloat16 [8, 4, 4, 2, 384, 384], P('kt', None, 'slab')
Inputs may be any that keep to these rules, and one draw needn't show every extreme that they name: neighbours[k, 0] is k - 1 or k - 2 and neighbours[k, 1] is k + 1 or k + 2, modulo 8.
All inputs are finite; a program needn't handle non-finite values.
Results may differ from a plain program's by a relative error of at most 0.017.
Values may be sent and summed in bfloat16 or wider, within the bound.
A program may use at most 128 MiB of HBM per device.

v0:
```python
import jax
import jax.numpy as jnp
from jax import lax
from jax.sharding import PartitionSpec as P

broaden = 0.05
fermi_level = 0.0
thermal = 0.1


def from_behind(value, axis, by):
    peers = lax.axis_size(axis)
    return lax.ppermute(value, axis, [(i, (i + by) % peers) for i in range(peers)])


def as_sent(value):
    return jax.tree.map(lambda a: a.astype(jnp.bfloat16) if a.dtype == jnp.float32 else a, value)


def combine(pieces):
    real_part = pieces[..., 0, 0, :, :] - pieces[..., 1, 1, :, :]
    imaginary_part = pieces[..., 0, 1, :, :] + pieces[..., 1, 0, :, :]
    return jnp.stack([real_part, imaginary_part], axis=-3)


def complex_mul(first_op, second_op):
    return combine(
        jnp.einsum("pij,qjk->pqik", first_op, second_op, preferred_element_type=jnp.float32)
    )


def adjoint(matrix):
    return jnp.stack([matrix[0].T, -matrix[1].T])


def slab_update(boundary, energy, levels, hamilton, coupling, phonon):
    moved_blocks = combine(
        jnp.einsum("pij,sqjk->spqik", coupling, boundary, preferred_element_type=jnp.float32)
    ).astype(jnp.bfloat16)
    self_both = combine(
        jnp.einsum(
            "spij,qjk->spqik", moved_blocks, adjoint(coupling), preferred_element_type=jnp.float32
        )
    )
    self_retarded = self_both[0]
    self_lesser = self_both[1]
    identity = jnp.eye(levels.shape[0], dtype=jnp.float32)
    system_real = (
        (energy - levels)[:, None] * identity
        - hamilton[0].astype(jnp.float32)
        - self_retarded[0]
        - phonon[0, 0]
    )
    system_imaginary = (
        broaden * identity - hamilton[1].astype(jnp.float32) - self_retarded[1] - phonon[0, 1]
    )
    diagonal_real = jnp.diagonal(system_real)
    diagonal_imaginary = jnp.diagonal(system_imaginary)
    modulus = diagonal_real * diagonal_real + diagonal_imaginary * diagonal_imaginary
    inverse_real = diagonal_real / modulus
    inverse_imaginary = -diagonal_imaginary / modulus
    scaled_real = (
        inverse_real[:, None] * system_real - inverse_imaginary[:, None] * system_imaginary
    )
    scaled_imaginary = (
        inverse_real[:, None] * system_imaginary + inverse_imaginary[:, None] * system_real
    )
    sandwich_real = (
        scaled_real * inverse_real[None, :] - scaled_imaginary * inverse_imaginary[None, :]
    )
    sandwich_imaginary = (
        scaled_real * inverse_imaginary[None, :] + scaled_imaginary * inverse_real[None, :]
    )
    first_guess = jnp.stack(
        [
            2.0 * jnp.diag(inverse_real) - sandwich_real,
            2.0 * jnp.diag(inverse_imaginary) - sandwich_imaginary,
        ]
    )
    first_rounded = first_guess.astype(jnp.bfloat16)
    system_rounded = jnp.stack([system_real, system_imaginary]).astype(jnp.bfloat16)
    product = complex_mul(system_rounded, first_rounded).astype(jnp.bfloat16)
    retarded = (2.0 * first_guess - complex_mul(first_rounded, product)).astype(jnp.bfloat16)
    source = (phonon[1] + self_lesser).astype(jnp.bfloat16)
    halfway = complex_mul(retarded, source).astype(jnp.bfloat16)
    lesser = complex_mul(halfway, adjoint(retarded)).astype(jnp.bfloat16)
    return (retarded, lesser)


def sweep_energy(boundary, energy, phonon, level_all, hamilton_all, coupling_all):
    slab_count = level_all.shape[0]
    retarded_list = [None] * slab_count
    lesser_list = [None] * slab_count
    for slab_num in reversed(range(slab_count)):
        ret_block, les_block = slab_update(
            boundary,
            energy,
            level_all[slab_num],
            hamilton_all[slab_num],
            coupling_all[slab_num],
            phonon[slab_num],
        )
        retarded_list[slab_num] = ret_block
        lesser_list[slab_num] = les_block
        boundary = jnp.stack([ret_block, les_block])
    return (jnp.stack(retarded_list), jnp.stack(lesser_list), boundary)


def cycle_phonon(blocks, neighbours, mode_index, mode_strength):
    nearest = [from_behind(blocks, "kt", offset) for offset in (1, -1)]
    farther = [from_behind(blocks, "kt", offset) for offset in (2, -2)]
    kpoint = lax.axis_index("kt")
    cycle_size = lax.axis_size("kt")
    neighbour_pair = neighbours[0]
    behind = jnp.where(neighbour_pair[0] == (kpoint - 1) % cycle_size, nearest[0], farther[0])
    forward = jnp.where(neighbour_pair[1] == (kpoint + 1) % cycle_size, nearest[1], farther[1])
    mode_table = jnp.arange(mode_strength.shape[0], dtype=jnp.int32)
    strength = jnp.sum(
        jnp.where(mode_index[0][:, None] == mode_table[None, :], mode_strength[None, :], 0.0),
        axis=1,
    )
    return strength[0] * behind[0].astype(jnp.float32) + strength[1] * forward[0].astype(
        jnp.float32
    )


def starting_blocks(contact, energy_list):
    contact_block = contact[0]
    contact_float = contact_block.astype(jnp.float32)
    skew_part = jnp.stack(
        [contact_float[0] - contact_float[0].T, contact_float[1] + contact_float[1].T]
    )
    occupation = 1.0 / (1.0 + jnp.exp((energy_list - fermi_level) / thermal))
    energy_count = energy_list.shape[0]
    contact_lesser = (-occupation[:, None, None, None] * skew_part).astype(jnp.bfloat16)
    return jnp.stack(
        [jnp.broadcast_to(contact_block, (energy_count,) + contact_block.shape), contact_lesser],
        axis=1,
    )


def body(
    energies, onsite, hamiltonian, hopping, contact, previous, neighbours, mode_index, mode_strength
):
    position = lax.axis_index("slab")
    regrouped = lax.all_to_all(previous, "slab", split_axis=1, concat_axis=2, tiled=True)
    phonon_all = cycle_phonon(regrouped, neighbours, mode_index, mode_strength)
    level_whole = lax.all_gather(onsite, "slab", axis=1, tiled=True)
    hamilton_whole, coupling_whole = (
        lax.all_gather(hamiltonian, "slab", axis=1, tiled=True),
        lax.all_gather(hopping, "slab", axis=1, tiled=True),
    )
    local_count = regrouped.shape[1]
    local_energies = lax.dynamic_slice_in_dim(energies, position * local_count, local_count, 0)
    initial = starting_blocks(contact, local_energies)

    def run_whole(boundary, energy, phonon):
        return sweep_energy(
            boundary, energy, phonon, level_whole[0], hamilton_whole[0], coupling_whole[0]
        )

    retarded_local, lesser_local, unused = jax.vmap(run_whole)(initial, local_energies, phonon_all)
    retarded_all, lesser_all = (
        lax.all_to_all(
            as_sent(retarded_local[None]), "slab", split_axis=2, concat_axis=1, tiled=True
        ),
        lax.all_to_all(
            as_sent(lesser_local[None]), "slab", split_axis=2, concat_axis=1, tiled=True
        ),
    )
    return (retarded_all, lesser_all)


def solution(mesh):
    in_specs = (
        P(),
        P("kt", "slab", None),
        P("kt", "slab", None, None, None),
        P("kt", "slab", None, None, None),
        P("kt", None, None, None),
        P("kt", None, "slab", None, None, None, None),
        P("kt", None),
        P("kt", None),
        P(),
    )
    out_specs = (P("kt", None, "slab", None, None, None), P("kt", None, "slab", None, None, None))
    return jax.shard_map(body, mesh=mesh, in_specs=in_specs, out_specs=out_specs, check_vma=False)
```

profile of v0, /device:TPU:0, one launch (start us, length us, event | category | flops | bytes accessed | tf_op | source)
XLA Modules:
  0.0 600.2 jit_solution(12964308768972763994)
XLA Ops:
  7.9 6.7 %copy.286 = bf16[1,4,1,2,2,384,384]{5,6,4,3,2,0,1:T(8,128)(2,1)} copy(bf16[1,4,1,2,2,384,384]{6,5,4,3,2,1,0:T(8,128)(2,1)} %param.14) | data formatting | bytes 9437184 | tf_op args[5]
  14.6 5.1 all-to-all-start
  20.4 77.7 %all-to-all-done = bf16[1,4,1,2,2,384,384]{5,6,4,3,2,0,1:T(8,128)(2,1)} async-done(((bf16[1,4,1,2,2,384,384]{5,6,4,3,2,0,1:T(8,128)(2,1)}), bf16[1,4,1,2,2,384,384]{5,6,4,3,2,0,1:T(8,128)(2,1)}, u32[]{:S(2)}, u32[]{:S(2)}) %all-to-all-start) | async-done | bytes 4718624 | tf_op jit(solution)/shard_map/all_to_all | solution.py:146
  98.1 1.5 collective-permute-start
  99.6 1.5 collective-permute-start.1
  101.1 3.2 collective-permute-start.2
  111.6 5.2 all_gather.9
  119.0 1.8 fusion.322
  128.1 2.5 convolution_bitcast_fusion.7
  130.8 1.5 copy-done.23
  133.6 1.4 convolution_bitcast_fusion.6
  137.2 68.8 %collective-permute-done = bf16[1,1,4,2,2,384,384]{5,6,4,3,2,1,0:T(8,128)(2,1)} collective-permute-done((bf16[1,1,4,2,2,384,384]{5,6,4,3,2,1,0:T(8,128)(2,1)}, bf16[1,1,4,2,2,384,384]{5,6,4,3,2,1,0:T(8,128)(2,1)}, u32[]{:S(2)}, u32[]{:S(2)}) %collective-permute-start) | collective-permute-done | bytes 4718624 | tf_op jit(solution)/shard_map/ppermute | solution.py:13
  206.4 99.2 %collective-permute-done.2 = bf16[1,1,4,2,2,384,384]{5,6,4,3,2,1,0:T(8,128)(2,1)} collective-permute-done((bf16[1,1,4,2,2,384,384]{5,6,4,3,2,1,0:T(8,128)(2,1)}, bf16[1,1,4,2,2,384,384]{5,6,4,3,2,1,0:T(8,128)(2,1)}, u32[]{:S(2)}, u32[]{:S(2)}) %collective-permute-start.2) | collective-permute-done | bytes 4718624 | tf_op jit(solution)/shard_map/ppermute | solution.py:13
  305.6 101.7 %collective-permute-done.3 = bf16[1,1,4,2,2,384,384]{5,6,4,3,2,1,0:T(8,128)(2,1)} collective-permute-done((bf16[1,1,4,2,2,384,384]{5,6,4,3,2,1,0:T(8,128)(2,1)}, bf16[1,1,4,2,2,384,384]{5,6,4,3,2,1,0:T(8,128)(2,1)}, u32[]{:S(2)}, u32[]{:S(2)}) %collective-permute-start.3) | collective-permute-done | bytes 4718624 | tf_op jit(solution)/shard_map/ppermute | solution.py:13
  407.3 12.0 %add_bitcast_fusion = f32[1,4,2,2,384,384]{4,5,3,2,1,0:T(8,128)} fusion(bf16[1,1,4,2,2,384,384]{5,6,4,3,2,1,0:T(8,128)(2,1)} %collective-permute-done.2, bf16[1,1,4,2,2,384,384]{5,6,4,3,2,1,0:T(8,128)(2,1)} %collective-permute-done.3, f32[]{:T(128)} %bitcast.80, bf16[1,1,4,2,2,384,384]{5,6,4,3,2,1,0:T(8,128)(2,1)} %collective-permute-done, ...), kind=kLoop, calls=%fused_computation.8 | loop fusion | flops 16515072 | bytes 28311562 | tf_op jit(solution)/shard_map/add | solution.py:122
  419.3 6.6 %slice_bitcast_fusion = (f32[1,2,2,384,384]{3,4,2,1,0:T(8,128)S(1)}, f32[1,2,2,384,384]{3,4,2,1,0:T(8,128)}, f32[1,2,2,384,384]{3,4,2,1,0:T(8,128)}, f32[1,1,2,2,384,384]{4,5,3,2,1,0:T(8,128)S(1)}) fusion(f32[1,4,2,2,384,384]{4,5,3,2,1,0:T(8,128)} %add_bitcast_fusion), kind=kLoop, calls=%fused_computation.9 | loop fusion | bytes 18874368 | tf_op jit(solution)/shard_map/vmap()/squeeze | solution.py:101
  426.9 1.3 convert_bitcast_fusion.23
  428.3 1.5 fusion.107
  429.8 5.1 gather_fusion
  434.9 4.5 gather_fusion.1
  440.0 1.5 subtract_subtract_fusion.3
  448.2 2.5 convolution_bitcast_fusion.5
  451.8 1.4 convolution_bitcast_fusion.4
  456.1 1.4 convert_bitcast_fusion.21
  457.6 3.5 gather_fusion.3
  461.1 4.7 gather_fusion.2
  466.4 1.5 subtract_subtract_fusion.2
  474.6 2.5 convolution_bitcast_fusion.3
  478.3 1.4 convolution_bitcast_fusion.2
  482.5 1.3 convert_bitcast_fusion.19
  484.0 3.5 gather_fusion.5
  487.5 3.7 gather_fusion.4
  491.3 1.5 subtract_subtract_fusion.1
  499.4 2.5 convolution_bitcast_fusion.1
  503.1 1.4 convolution_bitcast_fusion
  506.2 1.3 convert_bitcast_fusion.17
  507.8 3.5 gather_fusion.7
  511.3 3.5 gather_fusion.6
  514.8 1.6 subtract_subtract_fusion
  518.3 1.5 copy-done.11
  523.7 1.6 maximum_bitcast_fusion.1
  525.3 4.6 all-to-all-start.2
  531.4 1.8 maximum_bitcast_fusion
  533.1 25.3 %all-to-all-done.2 = bf16[1,1,4,2,384,384]{4,5,3,1,0,2:T(8,128)(2,1)} async-done(((bf16[1,1,4,2,384,384]{4,5,3,1,0,2:T(8,128)(2,1)}), bf16[1,1,4,2,384,384]{4,5,3,1,0,2:T(8,128)(2,1)}, u32[]{:S(2)}, u32[]{:S(2)}) %all-to-all-start.2) | async-done | bytes 2359328 | tf_op jit(solution)/shard_map/all_to_all | solution.py:167
  558.5 3.6 all-to-all-start.1
  562.1 4.3 copy.358
  566.4 24.2 %all-to-all-done.1 = bf16[1,1,4,2,384,384]{4,5,3,1,0,2:T(8,128)(2,1)S(1)} async-done(((bf16[1,1,4,2,384,384]{4,5,3,1,0,2:T(8,128)(2,1)}), bf16[1,1,4,2,384,384]{4,5,3,1,0,2:T(8,128)(2,1)S(1)}, u32[]{:S(2)}, u32[]{:S(2)}) %all-to-all-start.1) | async-done | bytes 2359328 | tf_op jit(solution)/shard_map/all_to_all | solution.py:164
  590.5 2.6 copy.357
  (263 shorter events, 60.5 us)
Async XLA Ops:
  7.2 111.8 %all-gather.3.cloned.1.call-start = ((), (), s32[]{:S(2)}) async-start(), calls=%async_computation.3 | async-start | bytes 2949120 | tf_op jit(solution)/shard_map/all_gather | solution.py:150
  14.6 90.3 %copy-start.54 = (bf16[1,2,384,384]{3,2,1,0:T(8,128)(2,1)S(1)}, bf16[1,2,384,384]{3,2,1,0:T(8,128)(2,1)}, u32[]{:S(2)}) copy-start(bf16[1,2,384,384]{3,2,1,0:T(8,128)(2,1)} %param.13) | copy-start | bytes 1769476
  14.6 83.5 %all-to-all-start = ((bf16[1,4,1,2,2,384,384]{5,6,4,3,2,0,1:T(8,128)(2,1)}), bf16[1,4,1,2,2,384,384]{5,6,4,3,2,0,1:T(8,128)(2,1)}, u32[]{:S(2)}, u32[]{:S(2)}) async-start(bf16[1,4,1,2,2,384,384]{5,6,4,3,2,0,1:T(8,128)(2,1)} %copy.286), calls=%async_computation | async-start | bytes 9437184 | tf_op jit(solution)/shard_map/all_to_all | solution.py:146
  19.6 108.4 %all-gather.5.cloned.1.call-start = ((), (), s32[]{:S(2)}) async-start(), calls=%async_computation.4 | async-start | bytes 2949120 | tf_op jit(solution)/shard_map/all_gather | solution.py:151
  98.1 107.9 %collective-permute-start = (bf16[1,1,4,2,2,384,384]{5,6,4,3,2,1,0:T(8,128)(2,1)}, bf16[1,1,4,2,2,384,384]{5,6,4,3,2,1,0:T(8,128)(2,1)}, u32[]{:S(2)}, u32[]{:S(2)}) collective-permute-start(bf16[1,1,4,2,2,384,384]{5,6,4,3,2,1,0:T(8,128)(2,1)} %bitcast.79), channel_id=1, source_target_pairs={{0,1},{1,2},{2,3},{3,4},{4,5},{5,6},{6,7},{7,0},{8,9},{9,10},{10,1... | collective-permute-start | bytes 14155784 | tf_op jit(solution)/shard_map/ppermute | solution.py:13
  99.6 106.8 %collective-permute-start.1 = (bf16[1,1,4,2,2,384,384]{5,6,4,3,2,1,0:T(8,128)(2,1)}, bf16[1,1,4,2,2,384,384]{5,6,4,3,2,1,0:T(8,128)(2,1)}, u32[]{:S(2)}, u32[]{:S(2)}) collective-permute-start(bf16[1,1,4,2,2,384,384]{5,6,4,3,2,1,0:T(8,128)(2,1)} %bitcast.79), channel_id=1, source_target_pairs={{0,2},{1,3},{2,4},{3,5},{4,6},{5,7},{6,0},{7,1},{8,10},{9,11},{10,... | collective-permute-start | bytes 14155784 | tf_op jit(solution)/shard_map/ppermute | solution.py:13
  101.1 204.6 %collective-permute-start.2 = (bf16[1,1,4,2,2,384,384]{5,6,4,3,2,1,0:T(8,128)(2,1)}, bf16[1,1,4,2,2,384,384]{5,6,4,3,2,1,0:T(8,128)(2,1)}, u32[]{:S(2)}, u32[]{:S(2)}) collective-permute-start(bf16[1,1,4,2,2,384,384]{5,6,4,3,2,1,0:T(8,128)(2,1)} %bitcast.79), channel_id=1, source_target_pairs={{0,7},{1,0},{2,1},{3,2},{4,3},{5,4},{6,5},{7,6},{8,15},{9,8},{10,9... | collective-permute-start | bytes 14155784 | tf_op jit(solution)/shard_map/ppermute | solution.py:13
  104.3 303.0 %collective-permute-start.3 = (bf16[1,1,4,2,2,384,384]{5,6,4,3,2,1,0:T(8,128)(2,1)}, bf16[1,1,4,2,2,384,384]{5,6,4,3,2,1,0:T(8,128)(2,1)}, u32[]{:S(2)}, u32[]{:S(2)}) collective-permute-start(bf16[1,1,4,2,2,384,384]{5,6,4,3,2,1,0:T(8,128)(2,1)} %bitcast.79), channel_id=1, source_target_pairs={{0,6},{1,7},{2,0},{3,1},{4,2},{5,3},{6,4},{7,5},{8,14},{9,15},{10,... | collective-permute-start | bytes 14155784 | tf_op jit(solution)/shard_map/ppermute | solution.py:13
  108.0 1.6 copy-start.73
  108.0 3.5 copy-start.74
  108.1 8.7 %copy-start.76 = (f32[4]{0:T(128)S(1)}, f32[4]{0:T(128)}, u32[]{:S(2)}) copy-start(f32[4]{0:T(128)} %param.17) | copy-start | bytes 52
  108.1 8.7 %copy-start.77 = (s32[1,2]{1,0:T(1,128)S(1)}, s32[1,2]{1,0:T(1,128)}, u32[]{:S(2)}) copy-start(s32[1,2]{1,0:T(1,128)} %param.16) | copy-start | bytes 28
  130.7 1.7 copy-start.23
  137.2 288.9 %copy-start.22 = (f32[1,2,384,384]{2,3,1,0:T(8,128)}, f32[1,2,384,384]{2,3,1,0:T(8,128)S(1)}, u32[]{:S(2)}) copy-start(f32[1,2,384,384]{2,3,1,0:T(8,128)S(1)} %fusion.7) | copy-start | bytes 3538948
  426.0 2.2 copy-start.4
  434.9 5.2 copy-start.55
  440.0 1.5 copy-start.67
  443.2 1.8 copy-start.5
  443.2 2.1 copy-start.7
  447.5 3.1 copy-start.28
  453.5 2.5 copy-start.2
  453.5 2.5 copy-start.50
  453.5 2.6 copy-start.51
  461.1 5.3 copy-start.56
  466.4 1.5 copy-start.69
  469.6 1.8 copy-start.3
  469.6 2.1 copy-start.15
  473.9 3.2 copy-start.30
  479.9 2.5 copy-start
  479.9 2.5 copy-start.48
  479.9 2.6 copy-start.49
  487.5 3.7 copy-start.57
  491.2 1.5 copy-start.70
  491.2 1.5 copy-start.71
  494.4 1.8 copy-start.1
  494.4 2.1 copy-start.19
  498.7 3.2 copy-start.32
  504.7 1.5 copy-start.47
  514.8 1.7 copy-start.64
  514.8 1.7 copy-start.65
  518.1 1.7 copy-start.11
  518.1 2.0 copy-start.13
  518.3 2.9 copy-start.24
  518.3 2.9 copy-start.26
  525.3 4.7 copy-start.25
  525.3 4.7 copy-start.27
  525.3 33.2 %all-to-all-start.2 = ((bf16[1,1,4,2,384,384]{4,5,3,1,0,2:T(8,128)(2,1)}), bf16[1,1,4,2,384,384]{4,5,3,1,0,2:T(8,128)(2,1)}, u32[]{:S(2)}, u32[]{:S(2)}) async-start(bf16[1,1,4,2,384,384]{4,5,3,1,0,2:T(8,128)(2,1)} %maximum_bitcast_fusion.1), calls=%async_computation.2 | async-start | bytes 4718592 | tf_op jit(solution)/shard_map/all_to_all | solution.py:167
  558.5 32.1 %all-to-all-start.1 = ((bf16[1,1,4,2,384,384]{4,5,3,1,0,2:T(8,128)(2,1)}), bf16[1,1,4,2,384,384]{4,5,3,1,0,2:T(8,128)(2,1)S(1)}, u32[]{:S(2)}, u32[]{:S(2)}) async-start(bf16[1,1,4,2,384,384]{4,5,3,1,0,2:T(8,128)(2,1)} %maximum_bitcast_fusion), calls=%async_computation.1 | async-start | bytes 4718592 | tf_op jit(solution)/shard_map/all_to_all | solution.py:164
  (39 other events, 42.5 us)
Sparse Core Ops, SparseCore 0:
  9.5 38.0 all-gather.2
  49.2 35.9 all-gather.4
where the time goes:
time: 610 us; the launch traced here: 600 us
  waiting for transfers between devices  399 us (65%)
  local copies, waits for them, and re-layouts  91.8 us (15%)
  other arithmetic  38.7 us (6%)
  matrix products  28 us (5%)
  starting transfers between devices  20.2 us (3%)
  between operations  17.6 us (3%)
    ppermute x4, waiting for transfers between devices, from_behind(): lax.ppermute(value, axis, [(i, (i + by) % peers) for i in range(peers)])  270 us
    all_to_all x1, waiting for transfers between devices, body(): lax.all_to_all(previous, 'slab', split_axis=1, concat_axis=2, tiled=True)  77.7 us
    unnamed x168, local copies, waits for them, and re-layouts  47 us
    all_to_all x1, waiting for transfers between devices, body(): lax.all_to_all(as_sent(lesser_local[None]), 'slab', split_axis=2, concat_...  25.3 us
    all_to_all x1, waiting for transfers between devices, body(): lax.all_to_all(as_sent(retarded_local[None]), 'slab', split_axis=2, conca...  24.2 us
    gather x4, local copies, waits for them, and re-layouts, slab_update(): diagonal_real = jnp.diagonal(system_real)  16.9 us
    gather x4, local copies, waits for them, and re-layouts, slab_update(): diagonal_imaginary = jnp.diagonal(system_imaginary)  14.9 us
    dot_general x16, matrix products, complex_mul(): jnp.einsum('pij,qjk->pqik', first_op, second_op, preferred_element_type=j...  12.6 us
  transfers between devices with their start and end apart: 9, of which 7 were waited for; matrix products, arithmetic and copies ran while one was open for 6% of the time, Pallas kernels for 0%

commit v1 on v0

--- a/solution.py
+++ b/solution.py
@@ -6,6 +6,36 @@
 broaden = 0.05
 fermi_level = 0.0
 thermal = 0.1
+
+
+def obtain_waves_for(page, d0, u_in):
+    piece_now, far_arr = (page.shape[:d0], page.shape[d0 + 1 :])
+    e_now = jnp.moveaxis(page.reshape(*piece_now, u_in, -1, *far_arr), d0, 0)
+    return e_now
+
+
+def report_the_vector(w_in, where_dim):
+    w_in = jnp.moveaxis(w_in, 0, where_dim)
+    plain = w_in.shape
+    vec_out = w_in.reshape(
+        *plain[:where_dim], plain[where_dim] * plain[where_dim + 1], *plain[where_dim + 2 :]
+    )
+    return vec_out
+
+
+def obtain_digits(x_local, peer_axis, chunk, tile_in):
+    now = lax.axis_size(peer_axis)
+    heard, fresh = (now, lax.axis_index(peer_axis))
+    a_next = obtain_waves_for(x_local, chunk, heard)
+    by_place = [a_next[fresh]]
+    ix = 1
+    while ix < heard:
+        low = a_next[fresh ^ ix]
+        by_place.append(lax.ppermute(low, peer_axis, [(to_i, to_i ^ ix) for to_i in range(heard)]))
+        ix += 1
+    a_next = jnp.stack(by_place, 0)[fresh ^ jnp.arange(heard)]
+    val2 = report_the_vector(a_next, tile_in)
+    return val2
 
 
 def from_behind(value, axis, by):
@@ -164,9 +194,7 @@
         lax.all_to_all(
             as_sent(retarded_local[None]), "slab", split_axis=2, concat_axis=1, tiled=True
         ),
-        lax.all_to_all(
-            as_sent(lesser_local[None]), "slab", split_axis=2, concat_axis=1, tiled=True
-        ),
+        obtain_digits(as_sent(lesser_local[None]), "slab", 2, 1),
     )
     return (retarded_all, lesser_all)
 

time: 610 us -> 608 us (level)
    ppermute x0 -> x3, waiting for transfers between devices: none -> 44.9 us  [obtain_digits(): lax.ppermute(low, peer_axis, [(to_i, to_i ^ ix) for to_i in range(heard)])]
    all_to_all x1 -> x0, waiting for transfers between devices: 25.3 us -> none  [body(): lax.all_to_all(as_sent(lesser_local[None]), 'slab', split_axis=2, concat_...]
    all_to_all x1, waiting for transfers between devices: 24.2 us -> 0.01 us  [body(): lax.all_to_all(as_sent(retarded_local[None]), 'slab', split_axis=2, conca...]
    unnamed x168 -> x171, local copies, waits for them, and re-layouts: 47 us -> 45.2 us
  transfers between devices with their start and end apart: 9 -> 11, of which waited for: 7 -> 7; matrix products, arithmetic and copies ran while one was open for 6% -> 6% of each run, Pallas kernels for 0% -> 0%
where the time goes in v1:
time: 608 us; the launch traced here: 599 us
  waiting for transfers between devices  394 us (65%)
  local copies, waits for them, and re-layouts  95.6 us (16%)
  other arithmetic  39.1 us (6%)
  matrix products  28 us (5%)
  starting transfers between devices  19 us (3%)
  between operations  17.8 us (3%)
    ppermute x4, waiting for transfers between devices, from_behind(): lax.ppermute(value, axis, [(i, (i + by) % peers) for i in range(peers)])  270 us
    all_to_all x1, waiting for transfers between devices, body(): lax.all_to_all(previous, 'slab', split_axis=1, concat_axis=2, tiled=True)  77.7 us
    unnamed x171, local copies, waits for them, and re-layouts  45.2 us
    ppermute x3, waiting for transfers between devices, obtain_digits(): lax.ppermute(low, peer_axis, [(to_i, to_i ^ ix) for to_i in range(heard)])  44.9 us
    gather x4, local copies, waits for them, and re-layouts, slab_update(): diagonal_real = jnp.diagonal(system_real)  16.9 us
    gather x4, local copies, waits for them, and re-layouts, slab_update(): diagonal_imaginary = jnp.diagonal(system_imaginary)  15 us
    dot_general x16, matrix products, complex_mul(): jnp.einsum('pij,qjk->pqik', first_op, second_op, preferred_element_type=j...  12.6 us
  transfers between devices with their start and end apart: 11, of which 7 were waited for; matrix products, arithmetic and copies ran while one was open for 6% of the time, Pallas kernels for 0%

profile of v1, /device:TPU:0, one launch (start us, length us, event | category | flops | bytes accessed | tf_op | source)
XLA Modules:
  0.0 598.6 jit_solution(15862127723592241607)
XLA Ops:
  7.9 6.7 %copy.369 = bf16[1,4,1,2,2,384,384]{5,6,4,3,2,0,1:T(8,128)(2,1)} copy(bf16[1,4,1,2,2,384,384]{6,5,4,3,2,1,0:T(8,128)(2,1)} %param.14) | data formatting | bytes 9437184 | tf_op args[5]
  14.6 5.1 all-to-all-start
  20.4 77.7 %all-to-all-done = bf16[1,4,1,2,2,384,384]{5,6,4,3,2,0,1:T(8,128)(2,1)} async-done(((bf16[1,4,1,2,2,384,384]{5,6,4,3,2,0,1:T(8,128)(2,1)}), bf16[1,4,1,2,2,384,384]{5,6,4,3,2,0,1:T(8,128)(2,1)}, u32[]{:S(2)}, u32[]{:S(2)}) %all-to-all-start) | async-done | bytes 4718624 | tf_op jit(solution)/shard_map/all_to_all | solution.py:176
  98.1 1.5 collective-permute-start
  99.6 1.5 collective-permute-start.1
  101.1 3.2 collective-permute-start.2
  111.7 5.2 all_gather.9
  119.1 1.9 fusion.323
  128.2 2.5 convolution_bitcast_fusion.7
  130.9 1.5 copy-done.23
  133.7 1.4 convolution_bitcast_fusion.6
  137.3 68.7 %collective-permute-done = bf16[1,1,4,2,2,384,384]{5,6,4,3,2,1,0:T(8,128)(2,1)} collective-permute-done((bf16[1,1,4,2,2,384,384]{5,6,4,3,2,1,0:T(8,128)(2,1)}, bf16[1,1,4,2,2,384,384]{5,6,4,3,2,1,0:T(8,128)(2,1)}, u32[]{:S(2)}, u32[]{:S(2)}) %collective-permute-start) | collective-permute-done | bytes 4718624 | tf_op jit(solution)/shard_map/ppermute | solution.py:43
  206.4 99.2 %collective-permute-done.2 = bf16[1,1,4,2,2,384,384]{5,6,4,3,2,1,0:T(8,128)(2,1)} collective-permute-done((bf16[1,1,4,2,2,384,384]{5,6,4,3,2,1,0:T(8,128)(2,1)}, bf16[1,1,4,2,2,384,384]{5,6,4,3,2,1,0:T(8,128)(2,1)}, u32[]{:S(2)}, u32[]{:S(2)}) %collective-permute-start.2) | collective-permute-done | bytes 4718624 | tf_op jit(solution)/shard_map/ppermute | solution.py:43
  305.6 101.7 %collective-permute-done.3 = bf16[1,1,4,2,2,384,384]{5,6,4,3,2,1,0:T(8,128)(2,1)} collective-permute-done((bf16[1,1,4,2,2,384,384]{5,6,4,3,2,1,0:T(8,128)(2,1)}, bf16[1,1,4,2,2,384,384]{5,6,4,3,2,1,0:T(8,128)(2,1)}, u32[]{:S(2)}, u32[]{:S(2)}) %collective-permute-start.3) | collective-permute-done | bytes 4718624 | tf_op jit(solution)/shard_map/ppermute | solution.py:43
  407.3 12.0 %add_bitcast_fusion = f32[1,4,2,2,384,384]{4,5,3,2,1,0:T(8,128)} fusion(bf16[1,1,4,2,2,384,384]{5,6,4,3,2,1,0:T(8,128)(2,1)} %collective-permute-done.2, bf16[1,1,4,2,2,384,384]{5,6,4,3,2,1,0:T(8,128)(2,1)} %collective-permute-done.3, f32[]{:T(128)} %bitcast.80, bf16[1,1,4,2,2,384,384]{5,6,4,3,2,1,0:T(8,128)(2,1)} %collective-permute-done, ...), kind=kLoop, calls=%fused_computation.9 | loop fusion | flops 16515072 | bytes 28311562 | tf_op jit(solution)/shard_map/add | solution.py:152
  419.3 6.6 %slice_bitcast_fusion = (f32[1,2,2,384,384]{3,4,2,1,0:T(8,128)S(1)}, f32[1,2,2,384,384]{3,4,2,1,0:T(8,128)}, f32[1,2,2,384,384]{3,4,2,1,0:T(8,128)}, f32[1,1,2,2,384,384]{4,5,3,2,1,0:T(8,128)S(1)}) fusion(f32[1,4,2,2,384,384]{4,5,3,2,1,0:T(8,128)} %add_bitcast_fusion), kind=kLoop, calls=%fused_computation.10 | loop fusion | bytes 18874368 | tf_op jit(solution)/shard_map/vmap()/squeeze | solution.py:131
  426.9 1.4 convert_bitcast_fusion.23
  428.3 1.5 fusion.107
  429.8 5.1 gather_fusion
  434.9 4.6 gather_fusion.1
  440.2 1.5 subtract_subtract_fusion.3
  448.4 2.5 convolution_bitcast_fusion.5
  452.0 1.4 convolution_bitcast_fusion.4
  456.3 1.4 convert_bitcast_fusion.21
  457.8 3.5 gather_fusion.3
  461.3 4.7 gather_fusion.2
  466.6 1.5 subtract_subtract_fusion.2
  474.8 2.5 convolution_bitcast_fusion.3
  478.4 1.4 convolution_bitcast_fusion.2
  482.7 1.3 convert_bitcast_fusion.19
  484.2 3.5 gather_fusion.5
  487.7 3.7 gather_fusion.4
  491.5 1.5 subtract_subtract_fusion.1
  499.6 2.5 convolution_bitcast_fusion.1
  503.3 1.4 convolution_bitcast_fusion
  506.4 1.4 convert_bitcast_fusion.17
  508.0 3.5 gather_fusion.7
  511.5 3.5 gather_fusion.6
  515.0 1.6 subtract_subtract_fusion
  518.5 1.5 copy-done.11
  522.8 1.8 maximum_bitcast_fusion
  524.6 4.9 all-to-all-start.1
  534.5 1.7 collective-permute-start.5
  537.6 33.5 %collective-permute-done.5 = bf16[1,1,1,2,384,384]{5,4,3,2,1,0:T(8,128)(2,1)S(1)} collective-permute-done((bf16[1,1,1,2,384,384]{5,4,3,2,1,0:T(8,128)(2,1)S(1)}, bf16[1,1,1,2,384,384]{5,4,3,2,1,0:T(8,128)(2,1)S(1)}, u32[]{:S(2)}, u32[]{:S(2)}) %collective-permute-start.5) | collective-permute-done | bytes 589856 | tf_op jit(solution)/shard_map/ppermute | solution.py:34
  571.1 11.5 %collective-permute-done.6 = bf16[1,1,1,2,384,384]{5,4,3,2,1,0:T(8,128)(2,1)S(1)} collective-permute-done((bf16[1,1,1,2,384,384]{5,4,3,2,1,0:T(8,128)(2,1)}, bf16[1,1,1,2,384,384]{5,4,3,2,1,0:T(8,128)(2,1)S(1)}, u32[]{:S(2)}, u32[]{:S(2)}) %collective-permute-start.6) | collective-permute-done | bytes 589856 | tf_op jit(solution)/shard_map/ppermute | solution.py:34
  583.4 1.6 maximum_bitcast_fusion.1
  585.0 2.3 gather_fusion.8
  587.3 4.3 copy.444
  (279 shorter events, 65.2 us)
Async XLA Ops:
  7.2 111.9 %all-gather.3.cloned.1.call-start = ((), (), s32[]{:S(2)}) async-start(), calls=%async_computation.2 | async-start | bytes 2949120 | tf_op jit(solution)/shard_map/all_gather | solution.py:180
  14.6 90.2 %copy-start.54 = (bf16[1,2,384,384]{3,2,1,0:T(8,128)(2,1)S(1)}, bf16[1,2,384,384]{3,2,1,0:T(8,128)(2,1)}, u32[]{:S(2)}) copy-start(bf16[1,2,384,384]{3,2,1,0:T(8,128)(2,1)} %param.13) | copy-start | bytes 1769476
  14.6 83.5 %all-to-all-start = ((bf16[1,4,1,2,2,384,384]{5,6,4,3,2,0,1:T(8,128)(2,1)}), bf16[1,4,1,2,2,384,384]{5,6,4,3,2,0,1:T(8,128)(2,1)}, u32[]{:S(2)}, u32[]{:S(2)}) async-start(bf16[1,4,1,2,2,384,384]{5,6,4,3,2,0,1:T(8,128)(2,1)} %copy.369), calls=%async_computation | async-start | bytes 9437184 | tf_op jit(solution)/shard_map/all_to_all | solution.py:176
  19.7 108.5 %all-gather.5.cloned.1.call-start = ((), (), s32[]{:S(2)}) async-start(), calls=%async_computation.3 | async-start | bytes 2949120 | tf_op jit(solution)/shard_map/all_gather | solution.py:181
  98.1 107.9 %collective-permute-start = (bf16[1,1,4,2,2,384,384]{5,6,4,3,2,1,0:T(8,128)(2,1)}, bf16[1,1,4,2,2,384,384]{5,6,4,3,2,1,0:T(8,128)(2,1)}, u32[]{:S(2)}, u32[]{:S(2)}) collective-permute-start(bf16[1,1,4,2,2,384,384]{5,6,4,3,2,1,0:T(8,128)(2,1)} %bitcast.79), channel_id=1, source_target_pairs={{0,1},{1,2},{2,3},{3,4},{4,5},{5,6},{6,7},{7,0},{8,9},{9,10},{10,1... | collective-permute-start | bytes 14155784 | tf_op jit(solution)/shard_map/ppermute | solution.py:43
  99.6 106.8 %collective-permute-start.1 = (bf16[1,1,4,2,2,384,384]{5,6,4,3,2,1,0:T(8,128)(2,1)}, bf16[1,1,4,2,2,384,384]{5,6,4,3,2,1,0:T(8,128)(2,1)}, u32[]{:S(2)}, u32[]{:S(2)}) collective-permute-start(bf16[1,1,4,2,2,384,384]{5,6,4,3,2,1,0:T(8,128)(2,1)} %bitcast.79), channel_id=1, source_target_pairs={{0,2},{1,3},{2,4},{3,5},{4,6},{5,7},{6,0},{7,1},{8,10},{9,11},{10,... | collective-permute-start | bytes 14155784 | tf_op jit(solution)/shard_map/ppermute | solution.py:43
  101.1 204.6 %collective-permute-start.2 = (bf16[1,1,4,2,2,384,384]{5,6,4,3,2,1,0:T(8,128)(2,1)}, bf16[1,1,4,2,2,384,384]{5,6,4,3,2,1,0:T(8,128)(2,1)}, u32[]{:S(2)}, u32[]{:S(2)}) collective-permute-start(bf16[1,1,4,2,2,384,384]{5,6,4,3,2,1,0:T(8,128)(2,1)} %bitcast.79), channel_id=1, source_target_pairs={{0,7},{1,0},{2,1},{3,2},{4,3},{5,4},{6,5},{7,6},{8,15},{9,8},{10,9... | collective-permute-start | bytes 14155784 | tf_op jit(solution)/shard_map/ppermute | solution.py:43
  104.3 303.0 %collective-permute-start.3 = (bf16[1,1,4,2,2,384,384]{5,6,4,3,2,1,0:T(8,128)(2,1)}, bf16[1,1,4,2,2,384,384]{5,6,4,3,2,1,0:T(8,128)(2,1)}, u32[]{:S(2)}, u32[]{:S(2)}) collective-permute-start(bf16[1,1,4,2,2,384,384]{5,6,4,3,2,1,0:T(8,128)(2,1)} %bitcast.79), channel_id=1, source_target_pairs={{0,6},{1,7},{2,0},{3,1},{4,2},{5,3},{6,4},{7,5},{8,14},{9,15},{10,... | collective-permute-start | bytes 14155784 | tf_op jit(solution)/shard_map/ppermute | solution.py:43
  108.1 1.6 copy-start.75
  108.1 3.5 copy-start.76
  108.1 8.7 %copy-start.78 = (f32[4]{0:T(128)S(1)}, f32[4]{0:T(128)}, u32[]{:S(2)}) copy-start(f32[4]{0:T(128)} %param.17) | copy-start | bytes 52
  108.2 8.7 %copy-start.79 = (s32[1,2]{1,0:T(1,128)S(1)}, s32[1,2]{1,0:T(1,128)}, u32[]{:S(2)}) copy-start(s32[1,2]{1,0:T(1,128)} %param.16) | copy-start | bytes 28
  130.8 1.7 copy-start.23
  137.3 288.8 %copy-start.22 = (f32[1,2,384,384]{2,3,1,0:T(8,128)}, f32[1,2,384,384]{2,3,1,0:T(8,128)S(1)}, u32[]{:S(2)}) copy-start(f32[1,2,384,384]{2,3,1,0:T(8,128)S(1)} %fusion.7) | copy-start | bytes 3538948
  426.0 2.3 copy-start.4
  434.9 5.3 copy-start.55
  440.2 1.5 copy-start.67
  443.4 1.8 copy-start.5
  443.4 2.1 copy-start.7
  447.7 3.1 copy-start.28
  453.7 2.5 copy-start.2
  453.7 2.5 copy-start.50
  453.7 2.6 copy-start.51
  461.3 5.3 copy-start.56
  469.8 1.8 copy-start.3
  469.8 2.1 copy-start.15
  474.1 3.1 copy-start.30
  480.1 2.5 copy-start
  480.1 2.5 copy-start.48
  480.1 2.6 copy-start.49
  487.7 3.7 copy-start.57
  491.4 1.5 copy-start.70
  494.6 1.8 copy-start.1
  494.7 2.1 copy-start.19
  498.9 3.1 copy-start.32
  515.0 1.7 copy-start.64
  515.0 1.7 copy-start.65
  518.3 1.7 copy-start.11
  518.3 2.0 copy-start.13
  518.5 2.9 copy-start.24
  518.5 2.9 copy-start.26
  524.6 4.9 copy-start.25
  524.6 4.9 copy-start.27
  524.6 62.7 %all-to-all-start.1 = ((bf16[1,1,4,2,384,384]{4,5,3,1,0,2:T(8,128)(2,1)}), bf16[1,1,4,2,384,384]{4,5,3,1,0,2:T(8,128)(2,1)}, u32[]{:S(2)}, u32[]{:S(2)}) async-start(bf16[1,1,4,2,384,384]{4,5,3,1,0,2:T(8,128)(2,1)} %maximum_bitcast_fusion), calls=%async_computation.1 | async-start | bytes 4718592 | tf_op jit(solution)/shard_map/all_to_all | solution.py:194
  533.7 3.9 collective-permute-start.4
  534.5 36.6 %collective-permute-start.5 = (bf16[1,1,1,2,384,384]{5,4,3,2,1,0:T(8,128)(2,1)S(1)}, bf16[1,1,1,2,384,384]{5,4,3,2,1,0:T(8,128)(2,1)S(1)}, u32[]{:S(2)}, u32[]{:S(2)}) collective-permute-start(bf16[1,1,1,2,384,384]{5,4,3,2,1,0:T(8,128)(2,1)S(1)} %bitcast.1093), channel_id=1, source_target_pairs={{0,16},{8,24},{16,0},{24,8},{1,17},{9,25},{17,1},{25,9},{2,18},{10... | collective-permute-start | bytes 1769480 | tf_op jit(solution)/shard_map/ppermute | solution.py:34
  537.3 45.3 %collective-permute-start.6 = (bf16[1,1,1,2,384,384]{5,4,3,2,1,0:T(8,128)(2,1)}, bf16[1,1,1,2,384,384]{5,4,3,2,1,0:T(8,128)(2,1)S(1)}, u32[]{:S(2)}, u32[]{:S(2)}) collective-permute-start(bf16[1,1,1,2,384,384]{5,4,3,2,1,0:T(8,128)(2,1)} %bitcast.374), channel_id=1, source_target_pairs={{0,24},{8,16},{16,8},{24,0},{1,25},{9,17},{17,9},{25,1},{2,26},{10... | collective-permute-start | bytes 1769480 | tf_op jit(solution)/shard_map/ppermute | solution.py:34
  571.1 11.5 %copy-start.72 = (bf16[1,1,1,2,384,384]{5,4,3,2,1,0:T(8,128)(2,1)}, bf16[1,1,1,2,384,384]{5,4,3,2,1,0:T(8,128)(2,1)S(1)}, u32[]{:S(2)}) copy-start(bf16[1,1,1,2,384,384]{5,4,3,2,1,0:T(8,128)(2,1)S(1)} %collective-permute-done.5) | copy-start | bytes 1769476
  (43 other events, 47.8 us)
Sparse Core Ops, SparseCore 0:
  9.5 37.9 all-gather.2
  49.1 35.9 all-gather.4
